TPU v7x, 256 devices: a whole 4x4x8 slice. The times are simulated.
256 devices in a mesh: grp: 32 (over z, x_lo, core), freq: 8 (over x_hi, y).
Axes of the slice: x: 4 (x_hi: 2, x_lo: 2; x = x_hi * 2 + x_lo), y: 4, z: 8, core: 2. Of those that a mesh axis runs over, the one named last changes fastest.
Arguments:
- spectra: bfloat16 [8, 8192, 1024], P('freq', 'grp'), may hold values from -3000 to 3000
- valid: int32 [8192, 512], P('grp'), may hold values 0 or 1
- station_index: int32 [16], replicated, may hold values from 0 to 8191, as said below
Outputs:
- cross: bfloat16 [8, 2, 8192, 8192], P('freq', None, 'grp')
- station_gather: float32 [16, 8192, 256], P(None, 'grp', 'freq')
Inputs may be any that keep to these rules, and one draw needn't show every extreme that they name: `station_index`: 16 distinct channel numbers.
All inputs are finite; a program needn't handle non-finite values. No bound on the sum of `valid` on one device may be relied on, other than what follows from the above.
Results may differ from a plain program's by a relative error of at most 0.0056.
Values may be sent and summed in bfloat16 or wider, within the bound.
A program may use at most 128 MiB of HBM per device.

v0:
```python
import math
import jax
import jax.numpy as jnp
from jax import lax
from jax.sharding import Mesh
from jax.sharding import PartitionSpec as P

LAGS = 256
GRP = ("chip", "core")


def on_device(spectra, valid, station_index):
    bin_count, chan_count, double_width = spectra.shape
    window_count = double_width // 2
    spectrum_f32 = spectra.astype(jnp.float32)
    real_part = spectrum_f32[..., :window_count]
    imag_part = spectrum_f32[..., window_count:]
    local_power = jnp.sum(real_part * real_part + imag_part * imag_part, axis=0)
    band_power = lax.psum(local_power, "freq")
    freq_count = lax.axis_size("freq")
    total_bins = bin_count * freq_count
    factor = lax.rsqrt(band_power / total_bins + 1e-05) * valid.astype(jnp.float32)
    whitened = (spectrum_f32 * jnp.concatenate([factor, factor], axis=1)[None]).astype(jnp.bfloat16)
    swapped = jnp.concatenate([whitened[..., window_count:], -whitened[..., :window_count]], axis=2)
    stacked = jnp.concatenate([whitened, swapped], axis=1)
    scaling = 1.0 / math.sqrt(window_count)
    chip_count = lax.axis_size("chip")
    core_count = lax.axis_size("core")
    same_core = lax.all_gather(whitened, "chip", axis=1)
    both_cores = lax.all_gather(same_core, "core", axis=2)
    peer_rows = both_cores.reshape(bin_count, chip_count * core_count * chan_count, double_width)
    product = jnp.einsum("bkw,bjw->bkj", stacked, peer_rows, preferred_element_type=jnp.float32)
    cross = (
        (product * scaling)
        .astype(jnp.bfloat16)
        .reshape(bin_count, 2, chan_count, peer_rows.shape[1])
    )
    station_count = station_index.shape[0]
    station_rows = jnp.take(peer_rows, station_index, axis=1)
    station_swapped = jnp.concatenate(
        [station_rows[..., window_count:], -station_rows[..., :window_count]], axis=2
    )
    station_left = jnp.concatenate([station_rows, station_swapped], axis=1)
    kernel = (
        jnp.einsum("bkw,bjw->bkj", station_left, whitened, preferred_element_type=jnp.float32)
        * scaling
    )
    kernel = kernel.reshape(bin_count, 2, station_count, chan_count)
    all_bins = lax.all_gather(kernel, "freq", axis=0, tiled=True)
    lag_share = LAGS // freq_count
    freq_index = lax.axis_index("freq")
    bin_values = jnp.arange(total_bins, dtype=jnp.float32) + 1.0
    lag_values = (freq_index * lag_share + jnp.arange(lag_share, dtype=jnp.int32)).astype(
        jnp.float32
    )
    phase = math.pi * bin_values[:, None] * lag_values[None, :] / LAGS
    lag_table = jnp.stack([jnp.cos(phase), -jnp.sin(phase)], axis=1)
    station_gather = jnp.einsum(
        "frsc,frl->scl", all_bins, lag_table, precision=lax.Precision.HIGHEST
    ) / math.sqrt(total_bins)
    return (cross, station_gather)


def solution(mesh):
    grp_size, freq_size = mesh.devices.shape
    fine = Mesh(mesh.devices.reshape(grp_size // 2, 2, freq_size), ("chip", "core", "freq"))
    placed = (P("freq", GRP, None), P(GRP, None), P())
    return jax.shard_map(
        on_device,
        mesh=fine,
        in_specs=placed,
        out_specs=(P("freq", None, GRP, None), P(None, GRP, "freq")),
        check_vma=False,
    )
```

profile of v0, /device:TPU:8, one launch (start us, length us, event | category | flops | bytes accessed | tf_op | source)
XLA Modules:
  0.0 394.3 jit_solution(18342799320419296325)
XLA Ops:
  7.2 0.0 all-reduce.2.cloned.1.call-start
  7.2 1.1 convert_element_type.20
  8.4 0.9 fusion.8
  9.3 0.0 all-reduce.2.cloned.1.call-update
  9.3 0.0 all-gather.5.cloned.1.call-start
  9.3 91.7 %all-reduce.2.cloned.1.call-done = f32[256,512]{1,0:T(8,128)} async-done(((f32[256,512]{1,0:T(8,128)}), f32[256,512]{1,0:T(8,128)}) %all-reduce.2.cloned.1.call-update) | async-done | bytes 524304 | tf_op jit(solution)/shard_map/psum | solution.py:19
  101.1 1.3 convert_multiply_fusion
  102.4 2.0 fusion.2
  104.3 0.0 all-gather.5.cloned.1.call-update
  104.4 0.0 all-gather.7.cloned.1.call-start
  104.4 184.2 %all-gather.5.cloned.1.call-done = bf16[16,256,1024]{2,1,0:T(8,128)(2,1)} async-done(((bf16[1,256,1024]{2,1,0:T(8,128)(2,1)}), bf16[16,256,1024]{2,1,0:T(8,128)(2,1)}) %all-gather.5.cloned.1.call-update) | async-done | bytes 8388624 | tf_op jit(solution)/shard_map/all_gather | solution.py:29
  288.6 0.0 all-gather.7.cloned.1.call-update
  288.7 0.7 compare_select_fusion
  289.3 0.7 compare_and_fusion
  290.0 0.1 fusion.17
  290.1 1.1 fusion.21
  291.2 36.0 %all-gather.7.cloned.1.call-done = bf16[16,512,1024]{2,1,0:T(8,128)(2,1)} async-done(((bf16[16,256,1024]{2,1,0:T(8,128)(2,1)}), bf16[16,512,1024]{2,1,0:T(8,128)(2,1)}) %all-gather.7.cloned.1.call-update) | async-done | bytes 16777232 | tf_op jit(solution)/shard_map/all_gather | solution.py:30
  327.2 8.5 %gather_fusion = bf16[16,1024]{1,0:T(8,128)(2,1)S(1)} fusion(bf16[8192,1024]{1,0:T(8,128)(2,1)} %bitcast.32, s32[1024]{0:T(1024)S(1)} %pad_clamp_fusion), kind=kCustom, calls=%fused_computation | custom fusion | bytes 65600 | tf_op jit(solution)/shard_map/jit(_take)/gather | solution.py:39
  335.7 0.1 bitcast_select_fusion
  335.8 1.3 convolution_multiply_fusion
  337.1 34.6 %all_gather.19 = f32[8,2,16,256]{3,2,1,0:T(8,128)S(1)} all-gather(f32[1,2,16,256]{3,2,1,0:T(8,128)S(1)} %bitcast.31), channel_id=1, replica_groups=mesh['chip'=16,'core'=2,'freq'=8] {'freq'}, dimensions={0}, use_global_device_ids=true | all-gather | bytes 294912 | tf_op jit(solution)/shard_map/all_gather | solution.py:49
  371.7 14.5 %multiply_convert_fusion = bf16[512,8192]{1,0:T(8,128)(2,1)} fusion(bf16[8192,1024]{1,0:T(8,128)(2,1)} %bitcast.33, bf16[1,256,512]{2,1,0:T(8,128)(2,1)S(1)} %get-tuple-element.3, bf16[1,256,512]{2,1,0:T(8,128)(2,1)S(1)} %get-tuple-element.2, bf16[1,256,1024]{2,1,0:T(8,128)(2,1)} %fusion.2), kind=kOutput, calls=%fused_computation.1 | convolution fusion | flops 8601468928 | bytes 26214400 | tf_op jit(solution)/shard_map/bkw,bjw->bkj/dot_general | solution.py:32
  386.3 1.5 fusion
  (4 shorter events, 0.0 us)
Async XLA Ops:
  7.2 93.9 %all-reduce.2.cloned.1.call-start = ((), (), s32[]{:S(2)}) async-start(), calls=%async_computation | async-start | bytes 1048576 | tf_op jit(solution)/shard_map/psum | solution.py:19
  9.3 279.3 %all-gather.5.cloned.1.call-start = ((), (), s32[]{:S(2)}) async-start(), calls=%async_computation.1 | async-start | bytes 8912896 | tf_op jit(solution)/shard_map/all_gather | solution.py:29
  104.4 222.8 %all-gather.7.cloned.1.call-start = ((), (), s32[]{:S(2)}) async-start(), calls=%async_computation.2 | async-start | bytes 25165824 | tf_op jit(solution)/shard_map/all_gather | solution.py:30
Sparse Core Ops, SparseCore 0:
  11.2 89.8 all-reduce.1
  104.5 184.0 all-gather.4
  290.6 36.5 all-gather.6
where the time goes:
time: 395 us; the launch traced here: 394 us
  waiting for transfers between devices  312 us (79%)
  blocking collectives  34.6 us (9%)
  matrix products  17.3 us (4%)
  between operations  13.8 us (3%)
  local copies, waits for them, and re-layouts  8.53 us (2%)
  other arithmetic  7.93 us (2%)
    all_gather x1, waiting for transfers between devices, on_device(): same_core = lax.all_gather(whitened, 'chip', axis=1)  184 us
    psum x1, waiting for transfers between devices, on_device(): band_power = lax.psum(local_power, 'freq')  91.7 us
    all_gather x1, waiting for transfers between devices, on_device(): both_cores = lax.all_gather(same_core, 'core', axis=2)  36 us
    all_gather x1, blocking collectives, on_device(): all_bins = lax.all_gather(kernel, 'freq', axis=0, tiled=True)  34.6 us
    dot_general x1, matrix products, on_device(): jnp.einsum('bkw,bjw->bkj', stacked, peer_rows, preferred_element_type=jnp...  14.5 us
    gather x1, local copies, waits for them, and re-layouts, on_device(): station_rows = jnp.take(peer_rows, station_index, axis=1)  8.53 us
  transfers between devices with their start and end apart: 3, of which 3 were waited for; matrix products, arithmetic and copies ran while one was open for 1% of the time, Pallas kernels for 0%

commit v1 on v0

--- a/solution.py
+++ b/solution.py
@@ -46,7 +46,10 @@
         * scaling
     )
     kernel = kernel.reshape(bin_count, 2, station_count, chan_count)
-    all_bins = lax.all_gather(kernel, "freq", axis=0, tiled=True)
+    count = lax.axis_size("freq")
+    blocks = jnp.stack([kernel for _ in range(count)])
+    blocks = lax.all_to_all(blocks, "freq", split_axis=0, concat_axis=0)
+    all_bins = jnp.concatenate(blocks, axis=0)
     lag_share = LAGS // freq_count
     freq_index = lax.axis_index("freq")
     bin_values = jnp.arange(total_bins, dtype=jnp.float32) + 1.0

time: 395 us -> 369 us (0.934)
  blocking collectives: 34.6 us -> 0 us
  starting transfers between devices: 0.12 us -> 7.36 us
    all_gather x1 -> x0, blocking collectives: 34.6 us -> none  [on_device(): all_bins = lax.all_gather(kernel, 'freq', axis=0, tiled=True)]
    all_to_all x0 -> x1, starting transfers between devices: none -> 7.24 us  [on_device(): blocks = lax.all_to_all(blocks, 'freq', split_axis=0, concat_axis=0)]
  transfers between devices with their start and end apart: 3 -> 4, of which waited for: 3 -> 3; matrix products, arithmetic and copies ran while one was open for 1% -> 5% of each run, Pallas kernels for 0% -> 0%
where the time goes in v1:
time: 369 us; the launch traced here: 368 us
  waiting for transfers between devices  312 us (85%)
  matrix products  17.3 us (5%)
  between operations  13.8 us (4%)
  local copies, waits for them, and re-layouts  9.34 us (3%)
  other arithmetic  7.93 us (2%)
  starting transfers between devices  7.36 us (2%)
    all_gather x1, waiting for transfers between devices, on_device(): same_core = lax.all_gather(whitened, 'chip', axis=1)  184 us
    psum x1, waiting for transfers between devices, on_device(): band_power = lax.psum(local_power, 'freq')  91.7 us
    all_gather x1, waiting for transfers between devices, on_device(): both_cores = lax.all_gather(same_core, 'core', axis=2)  36 us
    dot_general x1, matrix products, on_device(): jnp.einsum('bkw,bjw->bkj', stacked, peer_rows, preferred_element_type=jnp...  14.5 us
    gather x1, local copies, waits for them, and re-layouts, on_device(): station_rows = jnp.take(peer_rows, station_index, axis=1)  8.53 us
  transfers between devices with their start and end apart: 4, of which 3 were waited for; matrix products, arithmetic and copies ran while one was open for 5% of the time, Pallas kernels for 0%

profile of v1, /device:TPU:8, one launch (start us, length us, event | category | flops | bytes accessed | tf_op | source)
XLA Modules:
  0.0 367.7 jit_solution(8293517150846007481)
XLA Ops:
  7.2 0.0 all-reduce.2.cloned.1.call-start
  7.2 1.1 convert_element_type.20
  8.4 0.9 fusion.8
  9.3 0.0 all-reduce.2.cloned.1.call-update
  9.3 0.0 all-gather.5.cloned.1.call-start
  9.3 91.7 %all-reduce.2.cloned.1.call-done = f32[256,512]{1,0:T(8,128)} async-done(((f32[256,512]{1,0:T(8,128)}), f32[256,512]{1,0:T(8,128)}) %all-reduce.2.cloned.1.call-update) | async-done | bytes 524304 | tf_op jit(solution)/shard_map/psum | solution.py:19
  101.1 1.3 convert_multiply_fusion
  102.4 2.0 fusion.2
  104.3 0.0 all-gather.5.cloned.1.call-update
  104.4 0.0 all-gather.7.cloned.1.call-start
  104.4 184.2 %all-gather.5.cloned.1.call-done = bf16[16,256,1024]{2,1,0:T(8,128)(2,1)} async-done(((bf16[1,256,1024]{2,1,0:T(8,128)(2,1)}), bf16[16,256,1024]{2,1,0:T(8,128)(2,1)}) %all-gather.5.cloned.1.call-update) | async-done | bytes 8388624 | tf_op jit(solution)/shard_map/all_gather | solution.py:29
  288.6 0.0 all-gather.7.cloned.1.call-update
  288.7 0.7 compare_select_fusion
  289.3 0.7 compare_and_fusion
  290.0 0.1 fusion.18
  290.1 1.1 fusion.22
  291.2 36.0 %all-gather.7.cloned.1.call-done = bf16[16,512,1024]{2,1,0:T(8,128)(2,1)} async-done(((bf16[16,256,1024]{2,1,0:T(8,128)(2,1)}), bf16[16,512,1024]{2,1,0:T(8,128)(2,1)}) %all-gather.7.cloned.1.call-update) | async-done | bytes 16777232 | tf_op jit(solution)/shard_map/all_gather | solution.py:30
  327.2 8.5 %gather_fusion = bf16[16,1024]{1,0:T(8,128)(2,1)S(1)} fusion(bf16[8192,1024]{1,0:T(8,128)(2,1)} %bitcast.35, s32[1024]{0:T(1024)S(1)} %pad_clamp_fusion), kind=kCustom, calls=%fused_computation | custom fusion | bytes 65600 | tf_op jit(solution)/shard_map/jit(_take)/gather | solution.py:39
  335.7 0.1 bitcast_select_fusion
  335.8 1.3 convolution_multiply_fusion
  337.1 0.8 stack.8
  337.9 7.2 %all-to-all-start = ((f32[8,1,2,16,256]{4,2,3,1,0:T(2,128)}), f32[8,1,2,16,256]{4,2,3,1,0:T(2,128)S(1)}, u32[]{:S(2)}, u32[]{:S(2)}) async-start(f32[8,1,2,16,256]{4,2,3,1,0:T(2,128)} %stack.8), calls=%async_computation | async-start | bytes 524288 | tf_op jit(solution)/shard_map/all_to_all | solution.py:51
  345.2 14.5 %multiply_convert_fusion = bf16[512,8192]{1,0:T(8,128)(2,1)} fusion(bf16[8192,1024]{1,0:T(8,128)(2,1)} %bitcast.36, bf16[1,256,512]{2,1,0:T(8,128)(2,1)S(1)} %get-tuple-element.3, bf16[1,256,512]{2,1,0:T(8,128)(2,1)S(1)} %get-tuple-element.2, bf16[1,256,1024]{2,1,0:T(8,128)(2,1)} %fusion.2), kind=kOutput, calls=%fused_computation.1 | convolution fusion | flops 8601468928 | bytes 26214400 | tf_op jit(solution)/shard_map/bkw,bjw->bkj/dot_general | solution.py:32
  359.7 1.5 fusion
  (6 shorter events, 0.1 us)
Async XLA Ops:
  7.2 93.9 %all-reduce.2.cloned.1.call-start = ((), (), s32[]{:S(2)}) async-start(), calls=%async_computation.1 | async-start | bytes 1048576 | tf_op jit(solution)/shard_map/psum | solution.py:19
  9.3 279.3 %all-gather.5.cloned.1.call-start = ((), (), s32[]{:S(2)}) async-start(), calls=%async_computation.2 | async-start | bytes 8912896 | tf_op jit(solution)/shard_map/all_gather | solution.py:29
  104.4 222.8 %all-gather.7.cloned.1.call-start = ((), (), s32[]{:S(2)}) async-start(), calls=%async_computation.3 | async-start | bytes 25165824 | tf_op jit(solution)/shard_map/all_gather | solution.py:30
  337.9 21.8 %all-to-all-start = ((f32[8,1,2,16,256]{4,2,3,1,0:T(2,128)}), f32[8,1,2,16,256]{4,2,3,1,0:T(2,128)S(1)}, u32[]{:S(2)}, u32[]{:S(2)}) async-start(f32[8,1,2,16,256]{4,2,3,1,0:T(2,128)} %stack.8), calls=%async_computation | async-start | bytes 524288 | tf_op jit(solution)/shard_map/all_to_all | solution.py:51
Sparse Core Ops, SparseCore 0:
  11.2 89.8 all-reduce.1
  104.5 184.0 all-gather.4
  290.6 36.5 all-gather.6
